TPU v7x, 32 devices: a whole 2x2x4 slice. The times are simulated.
32 devices in a mesh: gx: 8 (over y, x, core), gy: 4 (over z).
Axes of the slice: x: 2, y: 2, z: 4, core: 2. Of those that a mesh axis runs over, the one named last changes fastest.
Arguments:
- right_side: float32 [2, 128, 512], P(None, 'gx', 'gy'), may hold values from -160 to 160
- conductivity: float32 [128, 512], P('gx', 'gy'), may hold values from 0.2 to 5
- leaf_inverse: float32 [32, 16, 128, 128], P('gx', 'gy'), may hold values from -1 to 4, as said below
- front_basis: float32 [128, 512, 128], P('gx', 'gy'), may hold values from -0.25 to 0.25
- leaf_transfer: float32 [8, 4, 128, 128], P('gx', 'gy'), may hold values from -0.4375 to 0.4375
- node_transfer: float32 [8, 4, 4, 128, 128], P('gx', 'gy'), may hold values from -1 to 1, as said below
- leaf_front: float32 [8, 4, 128, 128], P('gx', 'gy'), may hold values from -1 to 1, as said below
- node_front: float32 [8, 4, 5, 128, 128], P('gx', 'gy'), may hold values from -1 to 1, as said below
Outputs:
- solution: float32 [2, 128, 512], P(None, 'gx', 'gy')
- residual: float32 [2, 128, 512], P(None, 'gx', 'gy')
- direction: float32 [2, 128, 512], P(None, 'gx', 'gy')
Inputs may be any that keep to these rules, and one draw needn't show every extreme that they name: `leaf_inverse`: every block is symmetric and positive definite. `leaf_front`: every matrix is symmetric and positive definite. `node_front`: every matrix is symmetric and positive definite; entry h - 1 is the same for all tiles covered by one node of level h. `node_transfer`: entry h - 1 is the same for all tiles covered by one node of level h.
All inputs are finite; a program needn't handle non-finite values.
Results may differ from a plain program's by a relative error of at most 0.0001.
Values sent between devices are 32-bit elements; how exact they have to be, the bound alone decides.
No kernel may reach another device: no remote copies, remote signals or barrier semaphores. Data moves between devices by JAX's collectives and lax.ppermute only.
A program may use at most 64 MiB of HBM per device.

v0:
```python
from functools import partial
import jax
import jax.numpy as jnp
from jax import lax
from jax.sharding import PartitionSpec as P

LBX = 4
LBY = 32
HIGHEST = lax.Precision.HIGHEST


def extended(cells, sides, width):
    for axis, dim in sides:
        count = lax.axis_size(axis)
        ends = count - 1
        head = lax.slice_in_dim(cells, 0, width, axis=dim)
        tail = lax.slice_in_dim(cells, cells.shape[dim] - width, cells.shape[dim], axis=dim)
        cells = jnp.concatenate(
            [
                lax.ppermute(tail, axis, [(i, (i + 1) % count) for i in range(ends)]),
                cells,
                lax.ppermute(head, axis, [((i + 1) % count, i) for i in range(ends)]),
            ],
            axis=dim,
        )
    return cells


def from_partner(value, axis, distance):
    mask = 2**distance
    pairs = [(source, source ^ mask) for source in range(lax.axis_size(axis))]
    return lax.ppermute(value, axis, pairs)


def operate_padded(padded, padded_k):
    extent_x = padded.shape[1] - 2
    extent_y = padded.shape[2] - 2
    center = padded[:, 1:-1, 1:-1]
    center_k = padded_k[1:-1, 1:-1]
    summed = jnp.zeros_like(center)
    for offset_x, offset_y in ((2, 1), (0, 1), (1, 2), (1, 0)):
        beside = padded[:, offset_x : offset_x + extent_x, offset_y : offset_y + extent_y]
        beside_k = padded_k[offset_x : offset_x + extent_x, offset_y : offset_y + extent_y]
        summed = summed + 0.5 * (center_k + beside_k) * (center - beside)
    return summed


def stencil(values, conductivity):
    stacked = jnp.concatenate([values, conductivity[None]], axis=0)
    padded = extended(stacked, (("gx", 1), ("gy", 2)), 1)
    return operate_padded(padded[:-1], padded[-1])


def leaf_apply(values, leaf_inverse):
    count_s, extent_x, extent_y = values.shape
    blocks_x = extent_x // LBX
    blocks_y = extent_y // LBY
    grouped = values.reshape(count_s, blocks_x, LBX, blocks_y, LBY).transpose(0, 1, 3, 2, 4)
    grouped = grouped.reshape(count_s, blocks_x, blocks_y, LBX * LBY)
    mapped = jnp.einsum("xyij,sxyj->sxyi", leaf_inverse, grouped, precision=HIGHEST)
    mapped = mapped.reshape(count_s, blocks_x, blocks_y, LBX, LBY).transpose(0, 1, 3, 2, 4)
    return mapped.reshape(count_s, extent_x, extent_y)


def spread_tree(coeffs, leaf_transfer, node_transfer, leaf_front, node_front):
    levels = lax.axis_size(("gx", "gy")).bit_length() - 1
    leaf_t = leaf_transfer[0, 0]
    leaf_f = leaf_front[0, 0]
    node_t = node_transfer[0, 0]
    node_f = node_front[0, 0]
    uppers = [coeffs]
    moving = jnp.dot(coeffs, leaf_t, precision=HIGHEST)
    for height in range(1, levels + 1):
        partner = from_partner(moving, ("gx", "gy"), height - 1)
        summed = moving + partner
        uppers.append(summed)
        if height < levels:
            moving = jnp.dot(summed, node_t[height - 1], precision=HIGHEST)
    downward = jnp.dot(uppers[levels], node_f[levels - 1], precision=HIGHEST)
    for height in range(levels, 1, -1):
        downward = jnp.dot(downward, node_t[height - 2].T, precision=HIGHEST) + jnp.dot(
            uppers[height - 1], node_f[height - 2], precision=HIGHEST
        )
    return jnp.dot(downward, leaf_t.T, precision=HIGHEST) + jnp.dot(
        coeffs, leaf_f, precision=HIGHEST
    )


def precondition(
    values, leaf_inverse, front_basis, leaf_transfer, node_transfer, leaf_front, node_front
):
    near = leaf_apply(values, leaf_inverse)
    coeffs = jnp.einsum("sab,abk->sk", values, front_basis, precision=HIGHEST)
    spread = spread_tree(coeffs, leaf_transfer, node_transfer, leaf_front, node_front)
    return near + jnp.einsum("sk,abk->sab", spread, front_basis, precision=HIGHEST)


def on_device(
    right_side,
    conductivity,
    leaf_inverse,
    front_basis,
    leaf_transfer,
    node_transfer,
    leaf_front,
    node_front,
):
    apply_inverse = partial(
        precondition,
        leaf_inverse=leaf_inverse,
        front_basis=front_basis,
        leaf_transfer=leaf_transfer,
        node_transfer=node_transfer,
        leaf_front=leaf_front,
        node_front=node_front,
    )
    first_z = apply_inverse(right_side)
    local_rz = jnp.sum(right_side * first_z, axis=(1, 2))
    rz_old = lax.psum(local_rz, ("gx", "gy"))
    applied = stencil(first_z, conductivity)
    curvature = lax.psum(jnp.sum(first_z * applied, axis=(1, 2)), ("gx", "gy"))
    step_size = (rz_old / curvature)[:, None, None]
    solution = step_size * first_z
    residual = right_side - step_size * applied
    second_z = first_z - step_size * apply_inverse(applied)
    rz_new = lax.psum(jnp.sum(residual * second_z, axis=(1, 2)), ("gx", "gy"))
    direction = second_z + (rz_new / rz_old)[:, None, None] * first_z
    return (solution, residual, direction)


def solution(mesh):
    return jax.shard_map(
        on_device,
        mesh=mesh,
        in_specs=(
            P(None, "gx", "gy"),
            P("gx", "gy"),
            P("gx", "gy", None, None),
            P("gx", "gy", None),
            P("gx", "gy", None, None),
            P("gx", "gy", None, None, None),
            P("gx", "gy", None, None),
            P("gx", "gy", None, None, None),
        ),
        out_specs=(P(None, "gx", "gy"), P(None, "gx", "gy"), P(None, "gx", "gy")),
        check_vma=False,
    )
```

profile of v0, /device:TPU:0, one launch (start us, length us, event | category | flops | bytes accessed | tf_op | source)
XLA Modules:
  0.0 145.0 jit_solution(14396985049537503632)
XLA Ops:
  0.7 1.2 copy-done
  1.9 1.3 convolution_bitcast_fusion.3
  3.4 3.1 %collective-permute-start = (f32[2,128]{1,0:T(2,128)S(1)}, f32[2,128]{1,0:T(2,128)S(1)}, u32[]{:S(2)}, u32[]{:S(2)}) collective-permute-start(f32[2,128]{1,0:T(2,128)S(1)} %fusion.56), channel_id=1, source_target_pairs={{0,1},{1,0},{2,3},{3,2},{4,5},{5,4},{6,7},{7,6},{8,9},{9,8},{10,11... | collective-permute-start | bytes 3080 | tf_op jit(solution)/shard_map/ppermute | solution.py:32
  6.4 1.6 %collective-permute-done = f32[2,128]{1,0:T(2,128)S(1)} collective-permute-done((f32[2,128]{1,0:T(2,128)S(1)}, f32[2,128]{1,0:T(2,128)S(1)}, u32[]{:S(2)}, u32[]{:S(2)}) %collective-permute-start) | collective-permute-done | bytes 1056 | tf_op jit(solution)/shard_map/ppermute | solution.py:32
  8.1 3.1 %collective-permute-start.1 = (f32[2,128]{1,0:T(2,128)S(1)}, f32[2,128]{1,0:T(2,128)S(1)}, u32[]{:S(2)}, u32[]{:S(2)}) collective-permute-start(f32[2,128]{1,0:T(2,128)S(1)} %fusion.48), channel_id=1, source_target_pairs={{0,2},{1,3},{2,0},{3,1},{4,6},{5,7},{6,4},{7,5},{8,10},{9,11},{10,... | collective-permute-start | bytes 3080 | tf_op jit(solution)/shard_map/ppermute | solution.py:32
  11.2 1.6 %collective-permute-done.1 = f32[2,128]{1,0:T(2,128)S(1)} collective-permute-done((f32[2,128]{1,0:T(2,128)S(1)}, f32[2,128]{1,0:T(2,128)S(1)}, u32[]{:S(2)}, u32[]{:S(2)}) %collective-permute-start.1) | collective-permute-done | bytes 1056 | tf_op jit(solution)/shard_map/ppermute | solution.py:32
  12.9 1.2 collective-permute-done.2
  14.2 1.8 %collective-permute-start.3 = (f32[2,128]{1,0:T(2,128)S(1)}, f32[2,128]{1,0:T(2,128)S(1)}, u32[]{:S(2)}, u32[]{:S(2)}) collective-permute-start(f32[2,128]{1,0:T(2,128)S(1)} %fusion.32), channel_id=1, source_target_pairs={{0,8},{1,9},{2,10},{3,11},{4,12},{5,13},{6,14},{7,15},{8,0},{9,1},... | collective-permute-start | bytes 3080 | tf_op jit(solution)/shard_map/ppermute | solution.py:32
  16.1 0.8 reshape.54
  17.0 0.8 collective-permute-done.3
  18.0 1.9 %collective-permute-start.4 = (f32[2,128]{1,0:T(2,128)S(1)}, f32[2,128]{1,0:T(2,128)S(1)}, u32[]{:S(2)}, u32[]{:S(2)}) collective-permute-start(f32[2,128]{1,0:T(2,128)S(1)} %fusion.24), channel_id=1, source_target_pairs={{0,16},{1,17},{2,18},{3,19},{4,20},{5,21},{6,22},{7,23},{8,24},{9,... | collective-permute-start | bytes 3080 | tf_op jit(solution)/shard_map/ppermute | solution.py:32
  19.9 1.7 %convolution_bitcast_fusion.1 = f32[2,4,4,128]{3,0,2,1:T(2,128)S(1)} fusion(f32[2,4,4,128]{3,0,2,1:T(2,128)S(1)} %reshape.55, f32[4,4,128,128]{3,2,1,0:T(8,128)S(1)} %copy-done.2), kind=kOutput, calls=%fused_computation.1 | convolution fusion | flops 6291456 | bytes 1081344 | tf_op jit(solution)/shard_map/xyij,sxyj->sxyi/dot_general | solution.py:60
  22.2 0.2 convolution_add_fusion.11
  22.6 0.2 convolution_add_fusion.10
  23.0 0.2 convolution_add_fusion.9
  23.4 0.2 convolution_add_fusion.8
  23.8 0.5 copy-done.6
  24.4 1.0 convolution_add_fusion.1
  25.4 1.3 collective-permute-start.6
  26.7 3.0 %collective-permute-start.5 = (f32[3,1,128]{2,0,1:T(4,128)S(1)}, f32[3,1,128]{2,0,1:T(4,128)S(1)}, u32[]{:S(2)}, u32[]{:S(2)}) collective-permute-start(f32[3,1,128]{2,0,1:T(4,128)S(1)} %get-tuple-element.19), channel_id=1, source_target_pairs={{0,4},{4,8},{8,12},{12,16},{16,20},{20,24},{24,28},{1,5},{5,9},{9,... | collective-permute-start | bytes 4616 | tf_op jit(solution)/shard_map/ppermute | solution.py:20
  29.8 0.8 collective-permute-done.5
  30.7 3.5 %collective-permute-start.7 = (f32[3,18,1]{2,0,1:T(4,128)S(1)}, f32[3,18,1]{2,0,1:T(4,128)S(1)}, u32[]{:S(2)}, u32[]{:S(2)}) collective-permute-start(f32[3,18,1]{2,0,1:T(4,128)S(1)} %get-tuple-element.14), channel_id=1, source_target_pairs={{0,1},{1,2},{2,3},{4,5},{5,6},{6,7},{8,9},{9,10},{10,11},{12,13},{... | collective-permute-start | bytes 656 | tf_op jit(solution)/shard_map/ppermute | solution.py:20
  34.2 1.3 collective-permute-start.8
  35.5 0.5 collective-permute-done.7
  36.0 4.2 %collective-permute-done.8 = f32[3,18,1]{2,0,1:T(4,128)S(1)} collective-permute-done((f32[3,18,1]{2,0,1:T(4,128)S(1)}, f32[3,18,1]{2,0,1:T(4,128)S(1)}, u32[]{:S(2)}, u32[]{:S(2)}) %collective-permute-start.8) | collective-permute-done | bytes 248 | tf_op jit(solution)/shard_map/ppermute | solution.py:22
  40.5 0.6 copy-done.5
  41.1 0.3 multiply_reduce_fusion.1
  41.4 0.6 convolution_bitcast_fusion.2
  42.2 1.6 %collective-permute-start.9 = (f32[2,128]{1,0:T(2,128)S(1)}, f32[2,128]{1,0:T(2,128)S(1)}, u32[]{:S(2)}, u32[]{:S(2)}) collective-permute-start(f32[2,128]{1,0:T(2,128)S(1)} %fusion.52), channel_id=1, source_target_pairs={{0,1},{1,0},{2,3},{3,2},{4,5},{5,4},{6,7},{7,6},{8,9},{9,8},{10,11... | collective-permute-start | bytes 3080 | tf_op jit(solution)/shard_map/ppermute | solution.py:32
  43.8 2.0 %collective-permute-done.9 = f32[2,128]{1,0:T(2,128)S(1)} collective-permute-done((f32[2,128]{1,0:T(2,128)S(1)}, f32[2,128]{1,0:T(2,128)S(1)}, u32[]{:S(2)}, u32[]{:S(2)}) %collective-permute-start.9) | collective-permute-done | bytes 1056 | tf_op jit(solution)/shard_map/ppermute | solution.py:32
  45.9 2.6 %collective-permute-start.10 = (f32[2,128]{1,0:T(2,128)S(1)}, f32[2,128]{1,0:T(2,128)S(1)}, u32[]{:S(2)}, u32[]{:S(2)}) collective-permute-start(f32[2,128]{1,0:T(2,128)S(1)} %fusion.44), channel_id=1, source_target_pairs={{0,2},{1,3},{2,0},{3,1},{4,6},{5,7},{6,4},{7,5},{8,10},{9,11},{10,... | collective-permute-start | bytes 3080 | tf_op jit(solution)/shard_map/ppermute | solution.py:32
  48.5 1.9 %collective-permute-done.10 = f32[2,128]{1,0:T(2,128)S(1)} collective-permute-done((f32[2,128]{1,0:T(2,128)S(1)}, f32[2,128]{1,0:T(2,128)S(1)}, u32[]{:S(2)}, u32[]{:S(2)}) %collective-permute-start.10) | collective-permute-done | bytes 1056 | tf_op jit(solution)/shard_map/ppermute | solution.py:32
  50.6 1.2 collective-permute-done.11
  51.9 3.0 %collective-permute-start.12 = (f32[2,128]{1,0:T(2,128)S(1)}, f32[2,128]{1,0:T(2,128)S(1)}, u32[]{:S(2)}, u32[]{:S(2)}) collective-permute-start(f32[2,128]{1,0:T(2,128)S(1)} %fusion.28), channel_id=1, source_target_pairs={{0,8},{1,9},{2,10},{3,11},{4,12},{5,13},{6,14},{7,15},{8,0},{9,1},... | collective-permute-start | bytes 3080 | tf_op jit(solution)/shard_map/ppermute | solution.py:32
  55.2 1.3 collective-permute-done.12
  56.6 3.0 %collective-permute-start.13 = (f32[2,128]{1,0:T(2,128)S(1)}, f32[2,128]{1,0:T(2,128)S(1)}, u32[]{:S(2)}, u32[]{:S(2)}) collective-permute-start(f32[2,128]{1,0:T(2,128)S(1)} %fusion.20), channel_id=1, source_target_pairs={{0,16},{1,17},{2,18},{3,19},{4,20},{5,21},{6,22},{7,23},{8,24},{9,... | collective-permute-start | bytes 3080 | tf_op jit(solution)/shard_map/ppermute | solution.py:32
  59.6 1.7 %convolution_bitcast_fusion = f32[2,4,4,128]{3,0,2,1:T(2,128)S(1)} fusion(f32[2,4,4,128]{3,0,2,1:T(2,128)S(1)} %reshape.59, f32[4,4,128,128]{3,2,1,0:T(8,128)S(1)} %copy-done.2), kind=kOutput, calls=%fused_computation | convolution fusion | flops 6291456 | bytes 1081344 | tf_op jit(solution)/shard_map/xyij,sxyj->sxyi/dot_general | solution.py:60
  61.3 39.4 %all-reduce = (f32[2]{0:T(128)S(1)}, f32[2]{0:T(128)S(1)}) all-reduce(f32[2]{0:T(128)S(1)} %get-tuple-element.7, f32[2]{0:T(128)S(1)} %get-tuple-element.6), channel_id=1, replica_groups=mesh['gx'=8,'gy'=4] {'gx','gy'}, use_global_device_ids=true, to_apply=%region_1.0 | all-reduce | flops 4 | bytes 32 | tf_op jit(solution)/shard_map/psum | solution.py:119
  101.4 0.2 convolution_add_fusion.6
  101.8 0.2 convolution_add_fusion.5
  102.2 0.2 convolution_add_fusion.4
  102.5 0.2 convolution_add_fusion.3
  102.9 0.2 fusion.2
  103.1 1.1 multiply_reduce_fusion
  104.2 38.9 %psum.23 = f32[2]{0:T(128)S(1)} all-reduce(f32[2]{0:T(128)S(1)} %get-tuple-element.10), channel_id=1, replica_groups=mesh['gx'=8,'gy'=4] {'gx','gy'}, use_global_device_ids=true, to_apply=%region_5.0 | all-reduce | flops 2 | bytes 16 | tf_op jit(solution)/shard_map/psum | solution.py:126
  143.2 0.6 copy.18
  143.8 0.6 copy.19
  144.4 0.6 copy.20
  (61 shorter events, 5.2 us)
Async XLA Ops:
  0.6 1.2 copy-start
  0.6 2.5 %copy-start.4 = (f32[1,1,128,128]{3,2,1,0:T(8,128)S(1)}, f32[1,1,128,128]{3,2,1,0:T(8,128)}, u32[]{:S(2)}) copy-start(f32[1,1,128,128]{3,2,1,0:T(8,128)} %param.12) | copy-start | bytes 196612
  0.7 7.3 %copy-start.1 = (f32[1,1,4,128,128]{4,3,2,1,0:T(8,128)S(1)}, f32[1,1,4,128,128]{4,3,2,1,0:T(8,128)}, u32[]{:S(2)}) copy-start(f32[1,1,4,128,128]{4,3,2,1,0:T(8,128)} %param.13) | copy-start | bytes 786436
  0.7 19.2 %copy-start.2 = (f32[4,4,128,128]{3,2,1,0:T(8,128)S(1)}, f32[4,4,128,128]{3,2,1,0:T(8,128)}, u32[]{:S(2)}) copy-start(f32[4,4,128,128]{3,2,1,0:T(8,128)} %param.10) | copy-start | bytes 3145732
  3.4 4.6 %collective-permute-start = (f32[2,128]{1,0:T(2,128)S(1)}, f32[2,128]{1,0:T(2,128)S(1)}, u32[]{:S(2)}, u32[]{:S(2)}) collective-permute-start(f32[2,128]{1,0:T(2,128)S(1)} %fusion.56), channel_id=1, source_target_pairs={{0,1},{1,0},{2,3},{3,2},{4,5},{5,4},{6,7},{7,6},{8,9},{9,8},{10,11... | collective-permute-start | bytes 3080 | tf_op jit(solution)/shard_map/ppermute | solution.py:32
  8.1 4.6 %collective-permute-start.1 = (f32[2,128]{1,0:T(2,128)S(1)}, f32[2,128]{1,0:T(2,128)S(1)}, u32[]{:S(2)}, u32[]{:S(2)}) collective-permute-start(f32[2,128]{1,0:T(2,128)S(1)} %fusion.48), channel_id=1, source_target_pairs={{0,2},{1,3},{2,0},{3,1},{4,6},{5,7},{6,4},{7,5},{8,10},{9,11},{10,... | collective-permute-start | bytes 3080 | tf_op jit(solution)/shard_map/ppermute | solution.py:32
  12.9 1.2 collective-permute-start.2
  14.2 3.6 %collective-permute-start.3 = (f32[2,128]{1,0:T(2,128)S(1)}, f32[2,128]{1,0:T(2,128)S(1)}, u32[]{:S(2)}, u32[]{:S(2)}) collective-permute-start(f32[2,128]{1,0:T(2,128)S(1)} %fusion.32), channel_id=1, source_target_pairs={{0,8},{1,9},{2,10},{3,11},{4,12},{5,13},{6,14},{7,15},{8,0},{9,1},... | collective-permute-start | bytes 3080 | tf_op jit(solution)/shard_map/ppermute | solution.py:32
  18.0 3.9 %collective-permute-start.4 = (f32[2,128]{1,0:T(2,128)S(1)}, f32[2,128]{1,0:T(2,128)S(1)}, u32[]{:S(2)}, u32[]{:S(2)}) collective-permute-start(f32[2,128]{1,0:T(2,128)S(1)} %fusion.24), channel_id=1, source_target_pairs={{0,16},{1,17},{2,18},{3,19},{4,20},{5,21},{6,22},{7,23},{8,24},{9,... | collective-permute-start | bytes 3080 | tf_op jit(solution)/shard_map/ppermute | solution.py:32
  19.9 2.0 %copy-start.3 = (f32[1,1,5,128,128]{4,3,2,1,0:T(8,128)S(1)}, f32[1,1,5,128,128]{4,3,2,1,0:T(8,128)}, u32[]{:S(2)}) copy-start(f32[1,1,5,128,128]{4,3,2,1,0:T(8,128)} %param.15) | copy-start | bytes 983044
  23.4 0.9 copy-start.6
  24.4 1.0 copy-start.7
  25.4 4.3 %collective-permute-start.6 = (f32[3,1,128]{2,0,1:T(4,128)S(1)}, f32[3,1,128]{2,0,1:T(4,128)S(1)}, u32[]{:S(2)}, u32[]{:S(2)}) collective-permute-start(f32[3,1,128]{2,0,1:T(4,128)S(1)} %get-tuple-element.20), channel_id=1, source_target_pairs={{4,0},{8,4},{12,8},{16,12},{20,16},{24,20},{28,24},{5,1},{9,5},{13... | collective-permute-start | bytes 4616 | tf_op jit(solution)/shard_map/ppermute | solution.py:22
  26.7 3.8 %collective-permute-start.5 = (f32[3,1,128]{2,0,1:T(4,128)S(1)}, f32[3,1,128]{2,0,1:T(4,128)S(1)}, u32[]{:S(2)}, u32[]{:S(2)}) collective-permute-start(f32[3,1,128]{2,0,1:T(4,128)S(1)} %get-tuple-element.19), channel_id=1, source_target_pairs={{0,4},{4,8},{8,12},{12,16},{16,20},{20,24},{24,28},{1,5},{5,9},{9,... | collective-permute-start | bytes 4616 | tf_op jit(solution)/shard_map/ppermute | solution.py:20
  30.7 5.3 %collective-permute-start.7 = (f32[3,18,1]{2,0,1:T(4,128)S(1)}, f32[3,18,1]{2,0,1:T(4,128)S(1)}, u32[]{:S(2)}, u32[]{:S(2)}) collective-permute-start(f32[3,18,1]{2,0,1:T(4,128)S(1)} %get-tuple-element.14), channel_id=1, source_target_pairs={{0,1},{1,2},{2,3},{4,5},{5,6},{6,7},{8,9},{9,10},{10,11},{12,13},{... | collective-permute-start | bytes 656 | tf_op jit(solution)/shard_map/ppermute | solution.py:20
  34.2 6.0 %collective-permute-start.8 = (f32[3,18,1]{2,0,1:T(4,128)S(1)}, f32[3,18,1]{2,0,1:T(4,128)S(1)}, u32[]{:S(2)}, u32[]{:S(2)}) collective-permute-start(f32[3,18,1]{2,0,1:T(4,128)S(1)} %get-tuple-element.13), channel_id=1, source_target_pairs={{1,0},{2,1},{3,2},{5,4},{6,5},{7,6},{9,8},{10,9},{11,10},{13,12},{... | collective-permute-start | bytes 656 | tf_op jit(solution)/shard_map/ppermute | solution.py:22
  40.4 0.7 copy-start.5
  42.2 3.6 %collective-permute-start.9 = (f32[2,128]{1,0:T(2,128)S(1)}, f32[2,128]{1,0:T(2,128)S(1)}, u32[]{:S(2)}, u32[]{:S(2)}) collective-permute-start(f32[2,128]{1,0:T(2,128)S(1)} %fusion.52), channel_id=1, source_target_pairs={{0,1},{1,0},{2,3},{3,2},{4,5},{5,4},{6,7},{7,6},{8,9},{9,8},{10,11... | collective-permute-start | bytes 3080 | tf_op jit(solution)/shard_map/ppermute | solution.py:32
  45.9 4.5 %collective-permute-start.10 = (f32[2,128]{1,0:T(2,128)S(1)}, f32[2,128]{1,0:T(2,128)S(1)}, u32[]{:S(2)}, u32[]{:S(2)}) collective-permute-start(f32[2,128]{1,0:T(2,128)S(1)} %fusion.44), channel_id=1, source_target_pairs={{0,2},{1,3},{2,0},{3,1},{4,6},{5,7},{6,4},{7,5},{8,10},{9,11},{10,... | collective-permute-start | bytes 3080 | tf_op jit(solution)/shard_map/ppermute | solution.py:32
  50.6 1.2 collective-permute-start.11
  51.9 4.6 %collective-permute-start.12 = (f32[2,128]{1,0:T(2,128)S(1)}, f32[2,128]{1,0:T(2,128)S(1)}, u32[]{:S(2)}, u32[]{:S(2)}) collective-permute-start(f32[2,128]{1,0:T(2,128)S(1)} %fusion.28), channel_id=1, source_target_pairs={{0,8},{1,9},{2,10},{3,11},{4,12},{5,13},{6,14},{7,15},{8,0},{9,1},... | collective-permute-start | bytes 3080 | tf_op jit(solution)/shard_map/ppermute | solution.py:32
  56.6 44.4 %collective-permute-start.13 = (f32[2,128]{1,0:T(2,128)S(1)}, f32[2,128]{1,0:T(2,128)S(1)}, u32[]{:S(2)}, u32[]{:S(2)}) collective-permute-start(f32[2,128]{1,0:T(2,128)S(1)} %fusion.20), channel_id=1, source_target_pairs={{0,16},{1,17},{2,18},{3,19},{4,20},{5,21},{6,22},{7,23},{8,24},{9,... | collective-permute-start | bytes 3080 | tf_op jit(solution)/shard_map/ppermute | solution.py:32
where the time goes:
time: 146 us; the launch traced here: 145 us
  blocking collectives  78.3 us (54%)
  starting transfers between devices  29.2 us (20%)
  waiting for transfers between devices  17 us (12%)
  matrix products  13.2 us (9%)
  local copies, waits for them, and re-layouts  5.87 us (4%)
    psum x1, blocking collectives, on_device(): rz_old = lax.psum(local_rz, ('gx', 'gy'))  39.4 us
    psum x1, blocking collectives, on_device(): rz_new = lax.psum(jnp.sum(residual * second_z, axis=(1, 2)), ('gx', 'gy'))  38.9 us
    ppermute x10, starting transfers between devices, from_partner(): return lax.ppermute(value, axis, pairs)  20.1 us
    ppermute x10, waiting for transfers between devices, from_partner(): return lax.ppermute(value, axis, pairs)  11.5 us
    ppermute x2, starting transfers between devices, extended(): lax.ppermute(tail, axis, [(i, (i + 1) % count) for i in range(ends)])  6.55 us
    ppermute x2, waiting for transfers between devices, extended(): lax.ppermute(head, axis, [((i + 1) % count, i) for i in range(ends)])  4.23 us
    unnamed x20, local copies, waits for them, and re-layouts  4.17 us
    dot_general x2, matrix products, leaf_apply(): jnp.einsum('xyij,sxyj->sxyi', leaf_inverse, grouped, precision=HIGHEST)  3.46 us
  transfers between devices with their start and end apart: 14, of which 11 were waited for; matrix products, arithmetic and copies ran while one was open for 4% of the time, Pallas kernels for 0%

commit v1 on v0

--- a/solution.py
+++ b/solution.py
@@ -116,7 +116,7 @@
     )
     first_z = apply_inverse(right_side)
     local_rz = jnp.sum(right_side * first_z, axis=(1, 2))
-    rz_old = lax.psum(local_rz, ("gx", "gy"))
+    rz_old = lax.psum(lax.psum(local_rz, "gy"), "gx")
     applied = stencil(first_z, conductivity)
     curvature = lax.psum(jnp.sum(first_z * applied, axis=(1, 2)), ("gx", "gy"))
     step_size = (rz_old / curvature)[:, None, None]

time: 146 us -> 168 us (1.15)
  blocking collectives: 78.3 us -> 100 us
    psum x1 -> x3, blocking collectives: 39.4 us -> 60.9 us  [the longest x1 37.8 us: on_device(): curvature = lax.psum(jnp.sum(first_z * applied, axis=(1, 2)), ('gx', 'gy'))]
  transfers between devices with their start and end apart: 14 -> 14, of which waited for: 11 -> 11; matrix products, arithmetic and copies ran while one was open for 4% -> 3% of each run, Pallas kernels for 0% -> 0%
where the time goes in v1:
time: 168 us; the launch traced here: 167 us
  blocking collectives  100 us (60%)
  starting transfers between devices  29.2 us (17%)
  waiting for transfers between devices  17 us (10%)
  matrix products  13.2 us (8%)
  local copies, waits for them, and re-layouts  5.87 us (3%)
    psum x1, blocking collectives, on_device(): rz_new = lax.psum(jnp.sum(residual * second_z, axis=(1, 2)), ('gx', 'gy'))  39.5 us
    psum x1, blocking collectives, on_device(): curvature = lax.psum(jnp.sum(first_z * applied, axis=(1, 2)), ('gx', 'gy'))  37.8 us
    psum x2, blocking collectives, on_device(): rz_old = lax.psum(lax.psum(local_rz, 'gy'), 'gx')  23 us
    ppermute x10, starting transfers between devices, from_partner(): return lax.ppermute(value, axis, pairs)  20.1 us
    ppermute x10, waiting for transfers between devices, from_partner(): return lax.ppermute(value, axis, pairs)  11.5 us
    ppermute x2, starting transfers between devices, extended(): lax.ppermute(tail, axis, [(i, (i + 1) % count) for i in range(ends)])  6.55 us
    ppermute x2, waiting for transfers between devices, extended(): lax.ppermute(head, axis, [((i + 1) % count, i) for i in range(ends)])  4.23 us
    unnamed x20, local copies, waits for them, and re-layouts  4.17 us
  transfers between devices with their start and end apart: 14, of which 11 were waited for; matrix products, arithmetic and copies ran while one was open for 3% of the time, Pallas kernels for 0%

profile of v1, /device:TPU:0, one launch (start us, length us, event | category | flops | bytes accessed | tf_op | source)
XLA Modules:
  0.0 167.2 jit_solution(12495824912442685644)
XLA Ops:
  0.7 1.2 copy-done
  1.9 1.3 convolution_bitcast_fusion.3
  3.4 3.1 %collective-permute-start = (f32[2,128]{1,0:T(2,128)S(1)}, f32[2,128]{1,0:T(2,128)S(1)}, u32[]{:S(2)}, u32[]{:S(2)}) collective-permute-start(f32[2,128]{1,0:T(2,128)S(1)} %fusion.56), channel_id=1, source_target_pairs={{0,1},{1,0},{2,3},{3,2},{4,5},{5,4},{6,7},{7,6},{8,9},{9,8},{10,11... | collective-permute-start | bytes 3080 | tf_op jit(solution)/shard_map/ppermute | solution.py:32
  6.4 1.6 collective-permute-done
  8.1 3.1 %collective-permute-start.1 = (f32[2,128]{1,0:T(2,128)S(1)}, f32[2,128]{1,0:T(2,128)S(1)}, u32[]{:S(2)}, u32[]{:S(2)}) collective-permute-start(f32[2,128]{1,0:T(2,128)S(1)} %fusion.48), channel_id=1, source_target_pairs={{0,2},{1,3},{2,0},{3,1},{4,6},{5,7},{6,4},{7,5},{8,10},{9,11},{10,... | collective-permute-start | bytes 3080 | tf_op jit(solution)/shard_map/ppermute | solution.py:32
  11.2 1.6 collective-permute-done.1
  12.9 1.2 collective-permute-done.2
  14.2 1.8 %collective-permute-start.3 = (f32[2,128]{1,0:T(2,128)S(1)}, f32[2,128]{1,0:T(2,128)S(1)}, u32[]{:S(2)}, u32[]{:S(2)}) collective-permute-start(f32[2,128]{1,0:T(2,128)S(1)} %fusion.32), channel_id=1, source_target_pairs={{0,8},{1,9},{2,10},{3,11},{4,12},{5,13},{6,14},{7,15},{8,0},{9,1},... | collective-permute-start | bytes 3080 | tf_op jit(solution)/shard_map/ppermute | solution.py:32
  16.1 0.8 reshape.54
  17.0 0.8 collective-permute-done.3
  18.0 1.9 %collective-permute-start.4 = (f32[2,128]{1,0:T(2,128)S(1)}, f32[2,128]{1,0:T(2,128)S(1)}, u32[]{:S(2)}, u32[]{:S(2)}) collective-permute-start(f32[2,128]{1,0:T(2,128)S(1)} %fusion.24), channel_id=1, source_target_pairs={{0,16},{1,17},{2,18},{3,19},{4,20},{5,21},{6,22},{7,23},{8,24},{9,... | collective-permute-start | bytes 3080 | tf_op jit(solution)/shard_map/ppermute | solution.py:32
  19.9 1.7 %convolution_bitcast_fusion.1 = f32[2,4,4,128]{3,0,2,1:T(2,128)S(1)} fusion(f32[2,4,4,128]{3,0,2,1:T(2,128)S(1)} %reshape.55, f32[4,4,128,128]{3,2,1,0:T(8,128)S(1)} %copy-done.2), kind=kOutput, calls=%fused_computation.1 | convolution fusion | flops 6291456 | bytes 1081344 | tf_op jit(solution)/shard_map/xyij,sxyj->sxyi/dot_general | solution.py:60
  22.2 0.2 convolution_add_fusion.11
  22.6 0.2 convolution_add_fusion.10
  23.0 0.2 convolution_add_fusion.9
  23.4 0.2 convolution_add_fusion.8
  23.8 0.5 copy-done.6
  24.4 1.0 convolution_add_fusion.1
  25.4 1.3 collective-permute-start.6
  26.7 3.0 %collective-permute-start.5 = (f32[3,1,128]{2,0,1:T(4,128)S(1)}, f32[3,1,128]{2,0,1:T(4,128)S(1)}, u32[]{:S(2)}, u32[]{:S(2)}) collective-permute-start(f32[3,1,128]{2,0,1:T(4,128)S(1)} %get-tuple-element.17), channel_id=1, source_target_pairs={{0,4},{4,8},{8,12},{12,16},{16,20},{20,24},{24,28},{1,5},{5,9},{9,... | collective-permute-start | bytes 4616 | tf_op jit(solution)/shard_map/ppermute | solution.py:20
  29.8 0.8 collective-permute-done.5
  30.7 3.5 %collective-permute-start.7 = (f32[3,18,1]{2,0,1:T(4,128)S(1)}, f32[3,18,1]{2,0,1:T(4,128)S(1)}, u32[]{:S(2)}, u32[]{:S(2)}) collective-permute-start(f32[3,18,1]{2,0,1:T(4,128)S(1)} %get-tuple-element.12), channel_id=1, source_target_pairs={{0,1},{1,2},{2,3},{4,5},{5,6},{6,7},{8,9},{9,10},{10,11},{12,13},{... | collective-permute-start | bytes 656 | tf_op jit(solution)/shard_map/ppermute | solution.py:20
  34.2 1.3 collective-permute-start.8
  35.5 0.5 collective-permute-done.7
  36.0 4.2 %collective-permute-done.8 = f32[3,18,1]{2,0,1:T(4,128)S(1)} collective-permute-done((f32[3,18,1]{2,0,1:T(4,128)S(1)}, f32[3,18,1]{2,0,1:T(4,128)S(1)}, u32[]{:S(2)}, u32[]{:S(2)}) %collective-permute-start.8) | collective-permute-done | bytes 248 | tf_op jit(solution)/shard_map/ppermute | solution.py:22
  40.5 0.6 copy-done.5
  41.1 0.3 multiply_reduce_fusion.1
  41.4 0.6 convolution_bitcast_fusion.2
  42.2 1.6 collective-permute-start.9
  43.8 2.0 %collective-permute-done.9 = f32[2,128]{1,0:T(2,128)S(1)} collective-permute-done((f32[2,128]{1,0:T(2,128)S(1)}, f32[2,128]{1,0:T(2,128)S(1)}, u32[]{:S(2)}, u32[]{:S(2)}) %collective-permute-start.9) | collective-permute-done | bytes 1056 | tf_op jit(solution)/shard_map/ppermute | solution.py:32
  45.9 2.6 %collective-permute-start.10 = (f32[2,128]{1,0:T(2,128)S(1)}, f32[2,128]{1,0:T(2,128)S(1)}, u32[]{:S(2)}, u32[]{:S(2)}) collective-permute-start(f32[2,128]{1,0:T(2,128)S(1)} %fusion.44), channel_id=1, source_target_pairs={{0,2},{1,3},{2,0},{3,1},{4,6},{5,7},{6,4},{7,5},{8,10},{9,11},{10,... | collective-permute-start | bytes 3080 | tf_op jit(solution)/shard_map/ppermute | solution.py:32
  48.5 1.9 %collective-permute-done.10 = f32[2,128]{1,0:T(2,128)S(1)} collective-permute-done((f32[2,128]{1,0:T(2,128)S(1)}, f32[2,128]{1,0:T(2,128)S(1)}, u32[]{:S(2)}, u32[]{:S(2)}) %collective-permute-start.10) | collective-permute-done | bytes 1056 | tf_op jit(solution)/shard_map/ppermute | solution.py:32
  50.6 1.2 collective-permute-done.11
  51.9 3.0 %collective-permute-start.12 = (f32[2,128]{1,0:T(2,128)S(1)}, f32[2,128]{1,0:T(2,128)S(1)}, u32[]{:S(2)}, u32[]{:S(2)}) collective-permute-start(f32[2,128]{1,0:T(2,128)S(1)} %fusion.28), channel_id=1, source_target_pairs={{0,8},{1,9},{2,10},{3,11},{4,12},{5,13},{6,14},{7,15},{8,0},{9,1},... | collective-permute-start | bytes 3080 | tf_op jit(solution)/shard_map/ppermute | solution.py:32
  55.2 1.3 collective-permute-done.12
  56.6 3.0 %collective-permute-start.13 = (f32[2,128]{1,0:T(2,128)S(1)}, f32[2,128]{1,0:T(2,128)S(1)}, u32[]{:S(2)}, u32[]{:S(2)}) collective-permute-start(f32[2,128]{1,0:T(2,128)S(1)} %fusion.20), channel_id=1, source_target_pairs={{0,16},{1,17},{2,18},{3,19},{4,20},{5,21},{6,22},{7,23},{8,24},{9,... | collective-permute-start | bytes 3080 | tf_op jit(solution)/shard_map/ppermute | solution.py:32
  59.6 1.7 %convolution_bitcast_fusion = f32[2,4,4,128]{3,0,2,1:T(2,128)S(1)} fusion(f32[2,4,4,128]{3,0,2,1:T(2,128)S(1)} %reshape.59, f32[4,4,128,128]{3,2,1,0:T(8,128)S(1)} %copy-done.2), kind=kOutput, calls=%fused_computation | convolution fusion | flops 6291456 | bytes 1081344 | tf_op jit(solution)/shard_map/xyij,sxyj->sxyi/dot_general | solution.py:60
  61.3 10.4 %psum.28 = f32[2]{0:T(128)S(1)} all-reduce(f32[2]{0:T(128)S(1)} %get-tuple-element.7), channel_id=1, replica_groups=mesh['gx'=8,'gy'=4] {'gy'}, use_global_device_ids=true, to_apply=%region_1.0 | all-reduce | flops 2 | bytes 16 | tf_op jit(solution)/shard_map/psum | solution.py:119
  71.7 37.8 %psum.30 = f32[2]{0:T(128)S(1)} all-reduce(f32[2]{0:T(128)S(1)} %get-tuple-element.6), channel_id=1, replica_groups=mesh['gx'=8,'gy'=4] {'gx','gy'}, use_global_device_ids=true, to_apply=%region_4.0 | all-reduce | flops 2 | bytes 16 | tf_op jit(solution)/shard_map/psum | solution.py:121
  109.6 12.7 %psum.29 = f32[2]{0:T(128)S(1)} all-reduce(f32[2]{0:T(128)S(1)} %psum.28), channel_id=1, replica_groups=mesh['gx'=8,'gy'=4] {'gx'}, use_global_device_ids=true, to_apply=%region_2.0 | all-reduce | flops 2 | bytes 16 | tf_op jit(solution)/shard_map/psum | solution.py:119
  123.2 0.2 convolution_add_fusion.5
  123.6 0.2 convolution_add_fusion.4
  124.0 0.2 convolution_add_fusion.3
  124.6 1.1 multiply_reduce_fusion
  125.7 39.5 %psum.31 = f32[2]{0:T(128)S(1)} all-reduce(f32[2]{0:T(128)S(1)} %get-tuple-element.8), channel_id=1, replica_groups=mesh['gx'=8,'gy'=4] {'gx','gy'}, use_global_device_ids=true, to_apply=%region_6.0 | all-reduce | flops 2 | bytes 16 | tf_op jit(solution)/shard_map/psum | solution.py:126
  165.3 0.6 copy.18
  166.0 0.6 copy.19
  166.6 0.6 copy.20
  (63 shorter events, 5.6 us)
Async XLA Ops:
  0.6 1.2 copy-start
  0.6 2.5 %copy-start.4 = (f32[1,1,128,128]{3,2,1,0:T(8,128)S(1)}, f32[1,1,128,128]{3,2,1,0:T(8,128)}, u32[]{:S(2)}) copy-start(f32[1,1,128,128]{3,2,1,0:T(8,128)} %param.12) | copy-start | bytes 196612
  0.7 7.3 %copy-start.1 = (f32[1,1,4,128,128]{4,3,2,1,0:T(8,128)S(1)}, f32[1,1,4,128,128]{4,3,2,1,0:T(8,128)}, u32[]{:S(2)}) copy-start(f32[1,1,4,128,128]{4,3,2,1,0:T(8,128)} %param.13) | copy-start | bytes 786436
  0.7 19.2 %copy-start.2 = (f32[4,4,128,128]{3,2,1,0:T(8,128)S(1)}, f32[4,4,128,128]{3,2,1,0:T(8,128)}, u32[]{:S(2)}) copy-start(f32[4,4,128,128]{3,2,1,0:T(8,128)} %param.10) | copy-start | bytes 3145732
  3.4 4.6 %collective-permute-start = (f32[2,128]{1,0:T(2,128)S(1)}, f32[2,128]{1,0:T(2,128)S(1)}, u32[]{:S(2)}, u32[]{:S(2)}) collective-permute-start(f32[2,128]{1,0:T(2,128)S(1)} %fusion.56), channel_id=1, source_target_pairs={{0,1},{1,0},{2,3},{3,2},{4,5},{5,4},{6,7},{7,6},{8,9},{9,8},{10,11... | collective-permute-start | bytes 3080 | tf_op jit(solution)/shard_map/ppermute | solution.py:32
  8.1 4.6 %collective-permute-start.1 = (f32[2,128]{1,0:T(2,128)S(1)}, f32[2,128]{1,0:T(2,128)S(1)}, u32[]{:S(2)}, u32[]{:S(2)}) collective-permute-start(f32[2,128]{1,0:T(2,128)S(1)} %fusion.48), channel_id=1, source_target_pairs={{0,2},{1,3},{2,0},{3,1},{4,6},{5,7},{6,4},{7,5},{8,10},{9,11},{10,... | collective-permute-start | bytes 3080 | tf_op jit(solution)/shard_map/ppermute | solution.py:32
  12.9 1.2 collective-permute-start.2
  14.2 3.6 %collective-permute-start.3 = (f32[2,128]{1,0:T(2,128)S(1)}, f32[2,128]{1,0:T(2,128)S(1)}, u32[]{:S(2)}, u32[]{:S(2)}) collective-permute-start(f32[2,128]{1,0:T(2,128)S(1)} %fusion.32), channel_id=1, source_target_pairs={{0,8},{1,9},{2,10},{3,11},{4,12},{5,13},{6,14},{7,15},{8,0},{9,1},... | collective-permute-start | bytes 3080 | tf_op jit(solution)/shard_map/ppermute | solution.py:32
  18.0 3.9 %collective-permute-start.4 = (f32[2,128]{1,0:T(2,128)S(1)}, f32[2,128]{1,0:T(2,128)S(1)}, u32[]{:S(2)}, u32[]{:S(2)}) collective-permute-start(f32[2,128]{1,0:T(2,128)S(1)} %fusion.24), channel_id=1, source_target_pairs={{0,16},{1,17},{2,18},{3,19},{4,20},{5,21},{6,22},{7,23},{8,24},{9,... | collective-permute-start | bytes 3080 | tf_op jit(solution)/shard_map/ppermute | solution.py:32
  19.9 2.0 %copy-start.3 = (f32[1,1,5,128,128]{4,3,2,1,0:T(8,128)S(1)}, f32[1,1,5,128,128]{4,3,2,1,0:T(8,128)}, u32[]{:S(2)}) copy-start(f32[1,1,5,128,128]{4,3,2,1,0:T(8,128)} %param.15) | copy-start | bytes 983044
  23.4 0.9 copy-start.6
  24.4 1.0 copy-start.7
  25.4 4.3 %collective-permute-start.6 = (f32[3,1,128]{2,0,1:T(4,128)S(1)}, f32[3,1,128]{2,0,1:T(4,128)S(1)}, u32[]{:S(2)}, u32[]{:S(2)}) collective-permute-start(f32[3,1,128]{2,0,1:T(4,128)S(1)} %get-tuple-element.18), channel_id=1, source_target_pairs={{4,0},{8,4},{12,8},{16,12},{20,16},{24,20},{28,24},{5,1},{9,5},{13... | collective-permute-start | bytes 4616 | tf_op jit(solution)/shard_map/ppermute | solution.py:22
  26.7 3.8 %collective-permute-start.5 = (f32[3,1,128]{2,0,1:T(4,128)S(1)}, f32[3,1,128]{2,0,1:T(4,128)S(1)}, u32[]{:S(2)}, u32[]{:S(2)}) collective-permute-start(f32[3,1,128]{2,0,1:T(4,128)S(1)} %get-tuple-element.17), channel_id=1, source_target_pairs={{0,4},{4,8},{8,12},{12,16},{16,20},{20,24},{24,28},{1,5},{5,9},{9,... | collective-permute-start | bytes 4616 | tf_op jit(solution)/shard_map/ppermute | solution.py:20
  30.7 5.3 %collective-permute-start.7 = (f32[3,18,1]{2,0,1:T(4,128)S(1)}, f32[3,18,1]{2,0,1:T(4,128)S(1)}, u32[]{:S(2)}, u32[]{:S(2)}) collective-permute-start(f32[3,18,1]{2,0,1:T(4,128)S(1)} %get-tuple-element.12), channel_id=1, source_target_pairs={{0,1},{1,2},{2,3},{4,5},{5,6},{6,7},{8,9},{9,10},{10,11},{12,13},{... | collective-permute-start | bytes 656 | tf_op jit(solution)/shard_map/ppermute | solution.py:20
  34.2 6.0 %collective-permute-start.8 = (f32[3,18,1]{2,0,1:T(4,128)S(1)}, f32[3,18,1]{2,0,1:T(4,128)S(1)}, u32[]{:S(2)}, u32[]{:S(2)}) collective-permute-start(f32[3,18,1]{2,0,1:T(4,128)S(1)} %get-tuple-element.11), channel_id=1, source_target_pairs={{1,0},{2,1},{3,2},{5,4},{6,5},{7,6},{9,8},{10,9},{11,10},{13,12},{... | collective-permute-start | bytes 656 | tf_op jit(solution)/shard_map/ppermute | solution.py:22
  40.4 0.7 copy-start.5
  42.2 3.6 %collective-permute-start.9 = (f32[2,128]{1,0:T(2,128)S(1)}, f32[2,128]{1,0:T(2,128)S(1)}, u32[]{:S(2)}, u32[]{:S(2)}) collective-permute-start(f32[2,128]{1,0:T(2,128)S(1)} %fusion.52), channel_id=1, source_target_pairs={{0,1},{1,0},{2,3},{3,2},{4,5},{5,4},{6,7},{7,6},{8,9},{9,8},{10,11... | collective-permute-start | bytes 3080 | tf_op jit(solution)/shard_map/ppermute | solution.py:32
  45.9 4.5 %collective-permute-start.10 = (f32[2,128]{1,0:T(2,128)S(1)}, f32[2,128]{1,0:T(2,128)S(1)}, u32[]{:S(2)}, u32[]{:S(2)}) collective-permute-start(f32[2,128]{1,0:T(2,128)S(1)} %fusion.44), channel_id=1, source_target_pairs={{0,2},{1,3},{2,0},{3,1},{4,6},{5,7},{6,4},{7,5},{8,10},{9,11},{10,... | collective-permute-start | bytes 3080 | tf_op jit(solution)/shard_map/ppermute | solution.py:32
  50.6 1.2 collective-permute-start.11
  51.9 4.6 %collective-permute-start.12 = (f32[2,128]{1,0:T(2,128)S(1)}, f32[2,128]{1,0:T(2,128)S(1)}, u32[]{:S(2)}, u32[]{:S(2)}) collective-permute-start(f32[2,128]{1,0:T(2,128)S(1)} %fusion.28), channel_id=1, source_target_pairs={{0,8},{1,9},{2,10},{3,11},{4,12},{5,13},{6,14},{7,15},{8,0},{9,1},... | collective-permute-start | bytes 3080 | tf_op jit(solution)/shard_map/ppermute | solution.py:32
  56.6 65.8 %collective-permute-start.13 = (f32[2,128]{1,0:T(2,128)S(1)}, f32[2,128]{1,0:T(2,128)S(1)}, u32[]{:S(2)}, u32[]{:S(2)}) collective-permute-start(f32[2,128]{1,0:T(2,128)S(1)} %fusion.20), channel_id=1, source_target_pairs={{0,16},{1,17},{2,18},{3,19},{4,20},{5,21},{6,22},{7,23},{8,24},{9,... | collective-permute-start | bytes 3080 | tf_op jit(solution)/shard_map/ppermute | solution.py:32
